TPU v7x, 32 devices: a whole 2x2x4 slice. The times are simulated.
32 devices in a mesh: grp: 4 (over x, core), env: 8 (over z, y).
Axes of the slice: x: 2, y: 2, z: 4, core: 2. Of those that a mesh axis runs over, the one named last changes fastest.
Arguments:
- wavefunction: bfloat16 [8192, 1024], P('grp', 'env'), may hold values from -6 to 6
- left_tiles: bfloat16 [512, 128, 128], P(('grp', 'env')), may hold values from -0.5 to 0.5
- right_tiles: bfloat16 [26, 1024, 128], P(None, 'env'), may hold values from -0.5 to 0.5
- term_source: int32 [512], P('grp'), may hold values from 0 to 63
- term_target: int32 [512], P('grp'), may hold values from 0 to 63
- right_index: int32 [512], P('grp'), may hold values from 0 to 25
- term_sector: int32 [512, 1], P('grp'), may hold values from 0 to 31; in each aligned block of 16 rows (0 to 15, 16 to 31, ...) at most 4 rows name the same one
- column_sector: int32 [8], replicated, may hold values from 0 to 31
Outputs:
- applied: bfloat16 [8192, 1024], P('grp', 'env')
Inputs may be any that keep to these rules, and one draw needn't show every extreme that they name: `term_sector`: within each aligned block of 16 terms (the terms of one device) no sector appears more than 4 times, and every sector appears somewhere.
All inputs are finite; a program needn't handle non-finite values.
Results may differ from a plain program's by a relative error of at most 0.009.
Values may be sent and summed in bfloat16 or wider, within the bound.
A program may use at most 64 MiB of HBM per device.

v0:
```python
import jax
import jax.numpy as jnp
from jax import lax
from jax.sharding import PartitionSpec as P

MAXS = 4


def contribute(
    running, left_pick, source_rows, target_rows, right_rows, kept_mask, blocks, right_tiles
):
    source_blocks = blocks[source_rows]
    block_product = jnp.einsum(
        "kab,kbc->kac", left_pick, source_blocks, preferred_element_type=jnp.float32
    ).astype(jnp.bfloat16)
    term_image = jnp.einsum(
        "kac,kcd->kad", block_product, right_tiles[right_rows], preferred_element_type=jnp.float32
    )
    term_image = term_image * kept_mask[:, None, None]
    return running.at[target_rows].add(term_image)


def shards(
    wavefunction,
    left_tiles,
    right_tiles,
    term_source,
    term_target,
    right_index,
    term_sector,
    column_sector,
):
    tile_size = left_tiles.shape[1]
    env_count = lax.axis_size("env")
    env_place = lax.axis_index("env")
    sectors = term_sector[:, 0]
    my_sector = column_sector[env_place]
    gathered = lax.all_gather(wavefunction, "grp", axis=0, tiled=True)
    block_count = gathered.shape[0] // tile_size
    blocks = gathered.reshape(block_count, tile_size, tile_size)
    running = jnp.zeros((block_count, tile_size, tile_size), jnp.float32)
    tiles_dev = left_tiles.shape[0]
    sector_grid = sectors.reshape(env_count, tiles_dev)
    own_sectors = sector_grid[env_place]
    outgoing_miss = (own_sectors[None, :] != column_sector[:, None]).astype(jnp.int32)
    outgoing_pick = jnp.argsort(outgoing_miss, axis=1, stable=True)[:, :MAXS]
    outgoing = left_tiles[outgoing_pick]
    incoming = lax.all_to_all(outgoing, "env", split_axis=0, concat_axis=0, tiled=True)
    incoming_miss = (sector_grid != my_sector).astype(jnp.int32)
    incoming_pick = jnp.argsort(incoming_miss, axis=1, stable=True)[:, :MAXS]
    chosen = (jnp.arange(env_count, dtype=jnp.int32)[:, None] * tiles_dev + incoming_pick).reshape(
        -1
    )
    kept_mask = (
        (1 - jnp.take_along_axis(incoming_miss, incoming_pick, axis=1))
        .reshape(-1)
        .astype(jnp.float32)
    )
    running = contribute(
        running,
        incoming.reshape(-1, tile_size, tile_size),
        term_source[chosen],
        term_target[chosen],
        right_index[chosen],
        kept_mask,
        blocks,
        right_tiles,
    )
    summed = lax.psum_scatter(
        running.reshape(block_count * tile_size, tile_size).astype(jnp.bfloat16),
        "grp",
        scatter_dimension=0,
        tiled=True,
    )
    return summed


def solution(mesh):
    placed = (
        P("grp", "env"),
        P(("grp", "env"), None, None),
        P(None, "env", None),
        P("grp"),
        P("grp"),
        P("grp"),
        P("grp", None),
        P(),
    )
    return jax.shard_map(
        shards, mesh=mesh, in_specs=placed, out_specs=P("grp", "env"), check_vma=False
    )
```

profile of v0, /device:TPU:0, one launch (start us, length us, event | category | flops | bytes accessed | tf_op | source)
XLA Modules:
  0.0 99.9 jit_solution(12645802424836200396)
XLA Ops:
  6.5 0.7 all-gather.2.cloned.1.call-update
  7.3 0.5 broadcast.147
  7.8 1.3 %reduce.3 = s32[128]{0:T(128)S(1)} reduce(s32[128,1]{0,1:T(1,128)} %param.14, s32[]{:T(128)} %broadcast.147), dimensions={1}, to_apply=%param.14.reduce_sub_computation.3 | reduce | bytes 1028 | tf_op args[6]
  9.2 0.7 compare_convert_fusion
  9.9 0.7 sort.32
  10.8 2.7 %gather_fusion.1 = bf16[32,128,128]{2,1,0:T(8,128)(2,1)} fusion(bf16[16,128,128]{2,1,0:T(8,128)(2,1)} %param.9, s32[1024]{0:T(1024)S(1)} %pad_clamp_fusion.2), kind=kCustom, calls=%fused_computation.1 | custom fusion | bytes 2097280 | tf_op jit(solution)/shard_map/gather | solution.py:47
  13.5 7.3 %all-to-all-start = ((bf16[8,4,128,128]{3,2,1,0:T(8,128)(2,1)}), bf16[8,4,128,128]{3,2,1,0:T(8,128)(2,1)S(1)}, u32[]{:S(2)}, u32[]{:S(2)}) async-start(bf16[8,4,128,128]{3,2,1,0:T(8,128)(2,1)} %bitcast.5), calls=%async_computation | async-start | bytes 2097152 | tf_op jit(solution)/shard_map/all_to_all | solution.py:48
  20.9 0.6 dynamic_slice.6
  21.5 0.6 compare_convert_fusion.1
  22.2 0.7 sort.31
  23.1 0.7 gather_fusion.6
  24.3 0.7 gather_fusion.4
  25.0 0.7 gather_fusion.2
  25.7 0.7 gather_fusion
  26.5 1.7 %gather_fusion.5 = bf16[32,128,128]{2,1,0:T(8,128)(2,1)} fusion(bf16[26,128,128]{2,1,0:T(8,128)(2,1)S(1)} %copy-done, s32[1024]{0:T(1024)S(1)} %pad_clamp_fusion), kind=kCustom, calls=%fused_computation.5 | custom fusion | bytes 2097280 | tf_op jit(solution)/shard_map/gather | solution.py:17
  28.2 6.1 %all-gather.2.cloned.1.call-done = bf16[8192,128]{1,0:T(8,128)(2,1)} async-done(((bf16[2048,128]{1,0:T(8,128)(2,1)}), bf16[8192,128]{1,0:T(8,128)(2,1)}) %all-gather.2.cloned.1.call-update) | async-done | bytes 2097168 | tf_op jit(solution)/shard_map/all_gather | solution.py:38
  34.2 3.3 %gather_fusion.3 = bf16[32,128,128]{2,1,0:T(8,128)(2,1)} fusion(bf16[64,128,128]{2,1,0:T(8,128)(2,1)} %bitcast.31, s32[1024]{0:T(1024)S(1)} %pad_clamp_fusion.1), kind=kCustom, calls=%fused_computation.3 | custom fusion | bytes 2097280 | tf_op jit(solution)/shard_map/gather | solution.py:12
  37.5 9.1 %all-to-all-done = bf16[8,4,128,128]{3,2,1,0:T(8,128)(2,1)S(1)} async-done(((bf16[8,4,128,128]{3,2,1,0:T(8,128)(2,1)}), bf16[8,4,128,128]{3,2,1,0:T(8,128)(2,1)S(1)}, u32[]{:S(2)}, u32[]{:S(2)}) %all-to-all-start) | async-done | bytes 1048608 | tf_op jit(solution)/shard_map/all_to_all | solution.py:48
  46.6 1.0 copy-done.4
  47.6 2.6 %convolution_multiply_fusion = f32[32,128,128]{2,1,0:T(8,128)S(1)} fusion(bf16[32,128,128]{2,1,0:T(8,128)(2,1)} %gather_fusion.5, bf16[32,128,128]{2,1,0:T(8,128)(2,1)} %bitcast.30, bf16[32,128,128]{2,1,0:T(8,128)(2,1)} %gather_fusion.3, f32[32]{0:T(128)S(1)} %convert_element_type.29), kind=kOutput, calls=%fused_computation.8 | convolution fusion | flops 269484032 | bytes 5243008 | tf_op jit(solution)/shard_map/kac,kcd->kad/dot_general | solution.py:16
  50.2 2.4 %broadcast_in_dim.8 = f32[64,128,128]{2,1,0:T(8,128)} broadcast(f32[]{:T(128)} %constant.11.clone.1), dimensions={} | broadcast | bytes 4194308 | tf_op jit(solution)/shard_map/broadcast_in_dim | solution.py:41
  52.6 6.1 %scatter_fusion = f32[64,128,128]{2,1,0:T(8,128)} fusion(f32[64,128,128]{2,1,0:T(8,128)} %broadcast_in_dim.8, s32[32]{0:T(128)S(1)} %fusion.1, f32[32,128,128]{2,1,0:T(8,128)S(1)} %convolution_multiply_fusion), kind=kCustom, calls=%fused_computation.7 | custom fusion | flops 524288 | bytes 6291584 | tf_op jit(solution)/shard_map/scatter-add | solution.py:20
  58.7 3.9 %convert_element_type.30 = bf16[64,128,128]{2,1,0:T(8,128)(2,1)} convert(f32[64,128,128]{2,1,0:T(8,128)} %scatter_fusion) | non-fusion elementwise | flops 1048576 | bytes 6291456 | tf_op jit(solution)/shard_map/convert_element_type | solution.py:70
  62.7 30.4 %reduce-scatter.2.cloned.1.call-done = bf16[2048,128]{1,0:T(8,128)(2,1)} async-done(((bf16[8192,128]{1,0:T(8,128)(2,1)}), bf16[2048,128]{1,0:T(8,128)(2,1)}) %reduce-scatter.2.cloned.1.call-update) | async-done | bytes 524304 | tf_op jit(solution)/shard_map/reduce_scatter | solution.py:69
  (41 shorter events, 1.1 us)
Async XLA Ops:
  6.5 19.9 %copy-start = (bf16[26,128,128]{2,1,0:T(8,128)(2,1)S(1)}, bf16[26,128,128]{2,1,0:T(8,128)(2,1)}, u32[]{:S(2)}) copy-start(bf16[26,128,128]{2,1,0:T(8,128)(2,1)} %param.10) | copy-start | bytes 2555908
  6.5 27.7 %all-gather.2.cloned.1.call-start = ((), (), s32[]{:S(2)}) async-start(), calls=%async_computation.2 | async-start | bytes 2621440 | tf_op jit(solution)/shard_map/all_gather | solution.py:38
  10.8 10.1 %copy-start.5 = (s32[8]{0:T(128)S(1)}, s32[8]{0:T(128)}, u32[]{:S(2)}) copy-start(s32[8]{0:T(128)} %param.15) | copy-start | bytes 100
  13.5 33.1 %all-to-all-start = ((bf16[8,4,128,128]{3,2,1,0:T(8,128)(2,1)}), bf16[8,4,128,128]{3,2,1,0:T(8,128)(2,1)S(1)}, u32[]{:S(2)}, u32[]{:S(2)}) async-start(bf16[8,4,128,128]{3,2,1,0:T(8,128)(2,1)} %bitcast.5), calls=%async_computation | async-start | bytes 2097152 | tf_op jit(solution)/shard_map/all_to_all | solution.py:48
  20.8 72.2 %reduce-scatter.2.cloned.1.call-start = ((), (), s32[]{:S(2)}) async-start(), calls=%async_computation.3 | async-start | bytes 2621440 | tf_op jit(solution)/shard_map/reduce_scatter | solution.py:69
  23.1 1.2 %copy-start.1 = (s32[128]{0:T(128)S(1)}, s32[128]{0:T(128)}, u32[]{:S(2)}) copy-start(s32[128]{0:T(128)} %param.13) | copy-start | bytes 1540
  23.1 1.9 %copy-start.2 = (s32[128]{0:T(128)S(1)}, s32[128]{0:T(128)}, u32[]{:S(2)}) copy-start(s32[128]{0:T(128)} %param.11) | copy-start | bytes 1540
  23.1 2.6 %copy-start.3 = (s32[128]{0:T(128)S(1)}, s32[128]{0:T(128)}, u32[]{:S(2)}) copy-start(s32[128]{0:T(128)} %param.12) | copy-start | bytes 1540
  46.6 1.0 copy-start.4
Sparse Core Ops, SparseCore 0:
  8.9 25.2 all-gather.1
  62.8 30.2 reduce-scatter.1
where the time goes:
time: 100 us; the launch traced here: 99.9 us
  waiting for transfers between devices  46.3 us (46%)
  local copies, waits for them, and re-layouts  15.9 us (16%)
  other arithmetic  14.2 us (14%)
  between operations  13.5 us (14%)
  starting transfers between devices  7.35 us (7%)
  matrix products  2.57 us (3%)
    reduce_scatter x1, waiting for transfers between devices, shards(): lax.psum_scatter(running.reshape(block_count * tile_size, tile_size).asty...  30.4 us
    all_to_all x1, waiting for transfers between devices, shards(): lax.all_to_all(outgoing, 'env', split_axis=0, concat_axis=0, tiled=True)  9.13 us
    all_to_all x1, starting transfers between devices, shards(): lax.all_to_all(outgoing, 'env', split_axis=0, concat_axis=0, tiled=True)  7.31 us
    scatter-add x1, other arithmetic, contribute(): return running.at[target_rows].add(term_image)  6.13 us
    all_gather x1, waiting for transfers between devices, shards(): gathered = lax.all_gather(wavefunction, 'grp', axis=0, tiled=True)  6.05 us
    convert_element_type x1, other arithmetic, shards(): running.reshape(block_count * tile_size, tile_size).astype(jnp.bfloat16)  3.9 us
    gather x1, local copies, waits for them, and re-layouts, contribute(): source_blocks = blocks[source_rows]  3.25 us
    gather x1, local copies, waits for them, and re-layouts, shards(): outgoing = left_tiles[outgoing_pick]  2.7 us
  transfers between devices with their start and end apart: 3, of which 3 were waited for; matrix products, arithmetic and copies ran while one was open for 17% of the time, Pallas kernels for 0%

commit v1 on v0

--- a/solution.py
+++ b/solution.py
@@ -35,7 +35,14 @@
     env_place = lax.axis_index("env")
     sectors = term_sector[:, 0]
     my_sector = column_sector[env_place]
-    gathered = lax.all_gather(wavefunction, "grp", axis=0, tiled=True)
+    size = lax.axis_size("grp")
+    right = [(i, (i + 1) % size) for i in range(size)]
+    shards_2 = [wavefunction]
+    for far in range(1, size):
+        shards_2 = [lax.ppermute(shards_2[0], "grp", right), *shards_2]
+    full = jnp.concatenate(shards_2, axis=0)
+    places = (lax.axis_index("grp") + 1) * shards_2[-1].shape[0]
+    gathered = jnp.roll(full, places, axis=0)
     block_count = gathered.shape[0] // tile_size
     blocks = gathered.reshape(block_count, tile_size, tile_size)
     running = jnp.zeros((block_count, tile_size, tile_size), jnp.float32)

time: 100 us -> 99.7 us (level)
  local copies, waits for them, and re-layouts: 15.9 us -> 14.1 us
  starting transfers between devices: 7.35 us -> 8.84 us
    ppermute x0 -> x3, waiting for transfers between devices: none -> 11.7 us  [shards(): shards_2 = [lax.ppermute(shards_2[0], 'grp', right), *shards_2]]
    all_gather x1 -> x0, waiting for transfers between devices: 6.05 us -> none  [shards(): gathered = lax.all_gather(wavefunction, 'grp', axis=0, tiled=True)]
    all_to_all x1, waiting for transfers between devices: 9.13 us -> 4.58 us  [shards(): lax.all_to_all(outgoing, 'env', split_axis=0, concat_axis=0, tiled=True)]
    ppermute x0 -> x3, starting transfers between devices: none -> 1.85 us  [shards(): shards_2 = [lax.ppermute(shards_2[0], 'grp', right), *shards_2]]
    gather x1, local copies, waits for them, and re-layouts: 3.25 us -> 1.66 us  [contribute(): source_blocks = blocks[source_rows]]
  transfers between devices with their start and end apart: 3 -> 5, of which waited for: 3 -> 4; matrix products, arithmetic and copies ran while one was open for 17% -> 16% of each run, Pallas kernels for 0% -> 0%
where the time goes in v1:
time: 99.7 us; the launch traced here: 99.3 us
  waiting for transfers between devices  46.1 us (46%)
  other arithmetic  14.2 us (14%)
  local copies, waits for them, and re-layouts  14.1 us (14%)
  between operations  13.6 us (14%)
  starting transfers between devices  8.84 us (9%)
  matrix products  2.57 us (3%)
    reduce_scatter x1, waiting for transfers between devices, shards(): lax.psum_scatter(running.reshape(block_count * tile_size, tile_size).asty...  29.8 us
    ppermute x3, waiting for transfers between devices, shards(): shards_2 = [lax.ppermute(shards_2[0], 'grp', right), *shards_2]  11.7 us
    all_to_all x1, starting transfers between devices, shards(): lax.all_to_all(outgoing, 'env', split_axis=0, concat_axis=0, tiled=True)  6.95 us
    scatter-add x1, other arithmetic, contribute(): return running.at[target_rows].add(term_image)  6.13 us
    all_to_all x1, waiting for transfers between devices, shards(): lax.all_to_all(outgoing, 'env', split_axis=0, concat_axis=0, tiled=True)  4.58 us
    convert_element_type x1, other arithmetic, shards(): running.reshape(block_count * tile_size, tile_size).astype(jnp.bfloat16)  3.9 us
    gather x1, local copies, waits for them, and re-layouts, shards(): outgoing = left_tiles[outgoing_pick]  2.72 us
    dot_general x1, matrix products, contribute(): jnp.einsum('kac,kcd->kad', block_product, right_tiles[right_rows], prefer...  2.57 us
  transfers between devices with their start and end apart: 5, of which 4 were waited for; matrix products, arithmetic and copies ran while one was open for 16% of the time, Pallas kernels for 0%

profile of v1, /device:TPU:0, one launch (start us, length us, event | category | flops | bytes accessed | tf_op | source)
XLA Modules:
  0.0 99.3 jit_solution(17368790370751411037)
XLA Ops:
  7.0 0.5 broadcast.148
  7.5 1.3 %reduce.3 = s32[128]{0:T(128)S(1)} reduce(s32[128,1]{0,1:T(1,128)} %param.14, s32[]{:T(128)} %broadcast.148), dimensions={1}, to_apply=%param.14.reduce_sub_computation.3 | reduce | bytes 1028 | tf_op args[6]
  9.0 0.7 compare_convert_fusion
  9.7 0.7 sort.32
  10.6 2.7 %gather_fusion.1 = bf16[32,128,128]{2,1,0:T(8,128)(2,1)} fusion(bf16[16,128,128]{2,1,0:T(8,128)(2,1)} %param.9, s32[1024]{0:T(1024)S(1)} %pad_clamp_fusion.2), kind=kCustom, calls=%fused_computation.1 | custom fusion | bytes 2097280 | tf_op jit(solution)/shard_map/gather | solution.py:54
  13.3 7.0 %all-to-all-start = ((bf16[8,4,128,128]{3,2,1,0:T(8,128)(2,1)}), bf16[8,4,128,128]{3,2,1,0:T(8,128)(2,1)}, u32[]{:S(2)}, u32[]{:S(2)}) async-start(bf16[8,4,128,128]{3,2,1,0:T(8,128)(2,1)} %bitcast.5), calls=%async_computation | async-start | bytes 2097152 | tf_op jit(solution)/shard_map/all_to_all | solution.py:55
  20.3 0.6 dynamic_slice.10
  20.9 0.6 compare_convert_fusion.1
  21.6 0.7 sort.31
  22.5 0.7 gather_fusion.6
  23.4 1.4 %collective-permute-start.1 = (bf16[2048,128]{1,0:T(8,128)(2,1)S(1)}, bf16[2048,128]{1,0:T(8,128)(2,1)S(1)}, u32[]{:S(2)}, u32[]{:S(2)}) collective-permute-start(bf16[2048,128]{1,0:T(8,128)(2,1)S(1)} %collective-permute-done), channel_id=1, source_target_pairs={{0,8},{8,16},{16,24},{24,0},{1,9},{9,17},{17,25},{25,1},{2,10},{10... | collective-permute-start | bytes 1572872 | tf_op jit(solution)/shard_map/ppermute | solution.py:42
  24.9 0.7 gather_fusion.2
  25.6 0.7 gather_fusion.4
  26.3 5.7 %collective-permute-done.1 = bf16[2048,128]{1,0:T(8,128)(2,1)S(1)} collective-permute-done((bf16[2048,128]{1,0:T(8,128)(2,1)S(1)}, bf16[2048,128]{1,0:T(8,128)(2,1)S(1)}, u32[]{:S(2)}, u32[]{:S(2)}) %collective-permute-start.1) | collective-permute-done | bytes 524320 | tf_op jit(solution)/shard_map/ppermute | solution.py:42
  32.2 0.7 gather_fusion
  32.9 1.7 %gather_fusion.5 = bf16[32,128,128]{2,1,0:T(8,128)(2,1)} fusion(bf16[26,128,128]{2,1,0:T(8,128)(2,1)S(1)} %copy-done, s32[1024]{0:T(1024)S(1)} %pad_clamp_fusion), kind=kCustom, calls=%fused_computation.5 | custom fusion | bytes 2097280 | tf_op jit(solution)/shard_map/gather | solution.py:17
  34.6 6.0 %collective-permute-done.2 = bf16[2048,128]{1,0:T(8,128)(2,1)S(1)} collective-permute-done((bf16[2048,128]{1,0:T(8,128)(2,1)S(1)}, bf16[2048,128]{1,0:T(8,128)(2,1)S(1)}, u32[]{:S(2)}, u32[]{:S(2)}) %collective-permute-start.2) | collective-permute-done | bytes 524320 | tf_op jit(solution)/shard_map/ppermute | solution.py:42
  41.4 1.7 %gather_fusion.3 = bf16[32,128,128]{2,1,0:T(8,128)(2,1)} fusion(bf16[64,128,128]{2,1,0:T(8,128)(2,1)S(1)} %bitcast.30, s32[1024]{0:T(1024)S(1)} %pad_clamp_fusion.1), kind=kCustom, calls=%fused_computation.3 | custom fusion | bytes 2097280 | tf_op jit(solution)/shard_map/gather | solution.py:12
  43.0 4.6 %all-to-all-done = bf16[8,4,128,128]{3,2,1,0:T(8,128)(2,1)} async-done(((bf16[8,4,128,128]{3,2,1,0:T(8,128)(2,1)}), bf16[8,4,128,128]{3,2,1,0:T(8,128)(2,1)}, u32[]{:S(2)}, u32[]{:S(2)}) %all-to-all-start) | async-done | bytes 1048608 | tf_op jit(solution)/shard_map/all_to_all | solution.py:55
  47.6 2.6 %convolution_multiply_fusion = f32[32,128,128]{2,1,0:T(8,128)S(1)} fusion(bf16[32,128,128]{2,1,0:T(8,128)(2,1)} %gather_fusion.5, bf16[32,128,128]{2,1,0:T(8,128)(2,1)} %bitcast.6, bf16[32,128,128]{2,1,0:T(8,128)(2,1)} %gather_fusion.3, f32[32]{0:T(128)S(1)} %convert_element_type.29), kind=kOutput, calls=%fused_computation.8 | convolution fusion | flops 269484032 | bytes 5243008 | tf_op jit(solution)/shard_map/kac,kcd->kad/dot_general | solution.py:16
  50.2 2.4 %broadcast_in_dim.8 = f32[64,128,128]{2,1,0:T(8,128)} broadcast(f32[]{:T(128)} %constant.27.clone.1), dimensions={} | broadcast | bytes 4194308 | tf_op jit(solution)/shard_map/broadcast_in_dim | solution.py:48
  52.6 6.1 %scatter_fusion = f32[64,128,128]{2,1,0:T(8,128)} fusion(f32[64,128,128]{2,1,0:T(8,128)} %broadcast_in_dim.8, s32[32]{0:T(128)S(1)} %fusion.1, f32[32,128,128]{2,1,0:T(8,128)S(1)} %convolution_multiply_fusion), kind=kCustom, calls=%fused_computation.7 | custom fusion | flops 524288 | bytes 6291584 | tf_op jit(solution)/shard_map/scatter-add | solution.py:20
  58.7 3.9 %convert_element_type.30 = bf16[64,128,128]{2,1,0:T(8,128)(2,1)} convert(f32[64,128,128]{2,1,0:T(8,128)} %scatter_fusion) | non-fusion elementwise | flops 1048576 | bytes 6291456 | tf_op jit(solution)/shard_map/convert_element_type | solution.py:77
  62.7 29.8 %reduce-scatter.2.cloned.1.call-done = bf16[2048,128]{1,0:T(8,128)(2,1)} async-done(((bf16[8192,128]{1,0:T(8,128)(2,1)}), bf16[2048,128]{1,0:T(8,128)(2,1)}) %reduce-scatter.2.cloned.1.call-update) | async-done | bytes 524304 | tf_op jit(solution)/shard_map/reduce_scatter | solution.py:76
  (52 shorter events, 2.3 us)
Async XLA Ops:
  6.5 26.4 %copy-start = (bf16[26,128,128]{2,1,0:T(8,128)(2,1)S(1)}, bf16[26,128,128]{2,1,0:T(8,128)(2,1)}, u32[]{:S(2)}) copy-start(bf16[26,128,128]{2,1,0:T(8,128)(2,1)} %param.10) | copy-start | bytes 2555908
  6.5 13.8 %copy-start.5 = (s32[8]{0:T(128)S(1)}, s32[8]{0:T(128)}, u32[]{:S(2)}) copy-start(s32[8]{0:T(128)} %param.15) | copy-start | bytes 100
  6.5 16.8 %collective-permute-start = (bf16[2048,128]{1,0:T(8,128)(2,1)}, bf16[2048,128]{1,0:T(8,128)(2,1)S(1)}, u32[]{:S(2)}, u32[]{:S(2)}) collective-permute-start(bf16[2048,128]{1,0:T(8,128)(2,1)} %param.8), channel_id=1, source_target_pairs={{0,8},{8,16},{16,24},{24,0},{1,9},{9,17},{17,25},{25,1},{2,10},{10... | collective-permute-start | bytes 1572872 | tf_op jit(solution)/shard_map/ppermute | solution.py:42
  10.6 14.3 %copy-start.1 = (s32[128]{0:T(128)S(1)}, s32[128]{0:T(128)}, u32[]{:S(2)}) copy-start(s32[128]{0:T(128)} %param.11) | copy-start | bytes 1540
  10.6 15.0 %copy-start.2 = (s32[128]{0:T(128)S(1)}, s32[128]{0:T(128)}, u32[]{:S(2)}) copy-start(s32[128]{0:T(128)} %param.13) | copy-start | bytes 1540
  13.3 18.9 %copy-start.3 = (s32[128]{0:T(128)S(1)}, s32[128]{0:T(128)}, u32[]{:S(2)}) copy-start(s32[128]{0:T(128)} %param.12) | copy-start | bytes 1540
  13.3 34.3 %all-to-all-start = ((bf16[8,4,128,128]{3,2,1,0:T(8,128)(2,1)}), bf16[8,4,128,128]{3,2,1,0:T(8,128)(2,1)}, u32[]{:S(2)}, u32[]{:S(2)}) async-start(bf16[8,4,128,128]{3,2,1,0:T(8,128)(2,1)} %bitcast.5), calls=%async_computation | async-start | bytes 2097152 | tf_op jit(solution)/shard_map/all_to_all | solution.py:55
  20.3 72.2 %reduce-scatter.2.cloned.1.call-start = ((), (), s32[]{:S(2)}) async-start(), calls=%async_computation.2 | async-start | bytes 2621440 | tf_op jit(solution)/shard_map/reduce_scatter | solution.py:76
  23.2 17.6 %copy-start.4 = (bf16[2048,128]{1,0:T(8,128)(2,1)S(1)}, bf16[2048,128]{1,0:T(8,128)(2,1)}, u32[]{:S(2)}) copy-start(bf16[2048,128]{1,0:T(8,128)(2,1)} %param.8) | copy-start | bytes 1572868
  23.4 8.6 %collective-permute-start.1 = (bf16[2048,128]{1,0:T(8,128)(2,1)S(1)}, bf16[2048,128]{1,0:T(8,128)(2,1)S(1)}, u32[]{:S(2)}, u32[]{:S(2)}) collective-permute-start(bf16[2048,128]{1,0:T(8,128)(2,1)S(1)} %collective-permute-done), channel_id=1, source_target_pairs={{0,8},{8,16},{16,24},{24,0},{1,9},{9,17},{17,25},{25,1},{2,10},{10... | collective-permute-start | bytes 1572872 | tf_op jit(solution)/shard_map/ppermute | solution.py:42
  32.0 8.6 %collective-permute-start.2 = (bf16[2048,128]{1,0:T(8,128)(2,1)S(1)}, bf16[2048,128]{1,0:T(8,128)(2,1)S(1)}, u32[]{:S(2)}, u32[]{:S(2)}) collective-permute-start(bf16[2048,128]{1,0:T(8,128)(2,1)S(1)} %collective-permute-done.1), channel_id=1, source_target_pairs={{0,8},{8,16},{16,24},{24,0},{1,9},{9,17},{17,25},{25,1},{2,10},{10... | collective-permute-start | bytes 1572872 | tf_op jit(solution)/shard_map/ppermute | solution.py:42
Sparse Core Ops, SparseCore 0:
  62.8 29.6 reduce-scatter.1
